TPU v7x, 32 devices: a whole 2x2x4 slice. The times are simulated.
32 devices in a mesh: table: 16 (over z, y, x), mp: 2 (over core).
Axes of the slice: x: 2, y: 2, z: 4, core: 2. Of those that a mesh axis runs over, the one named last changes fastest.
Arguments:
- hash_tables: bfloat16 [2, 16384, 4096], P(None, 'table', 'mp'), may hold values from -6 to 6
- byte_table: bfloat16 [256, 4096], P(None, 'mp'), may hold values from -6 to 6
- byte_ids: int32 [4096], P('table'), may hold values from 0 to 255
- hash_owner: int32 [2, 4096, 1], P(None, 'table'), may hold values from 0 to 15; in each aligned block of 256 rows (0 to 255, 256 to 511, ..., all dimensions but the last counted through in order) at most 32 rows name the same one
- hash_offset: int32 [2, 4096], P(None, 'table'), may hold values from 0 to 1023
- gain: float32 [4096], replicated, may hold values from 0.25 to 1.75
- proj_weight: bfloat16 [4096, 4096], P('table', 'mp'), may hold values from -0.09375 to 0.09375
- cotangent: bfloat16 [4096, 4096], P('table', 'mp'), may hold values from -6 to 6
Outputs:
- projected: bfloat16 [4096, 4096], P('table', 'mp')
- table_grads: bfloat16 [2, 16384, 4096], P(None, 'table', 'mp')
Inputs may be any that keep to these rules, and one draw needn't show every extreme that they name: `hash_owner`: within the 256 bytes of one device and one table, no owner is named more than 32 times, a bound that some of these blocks reach.
All inputs are finite; a program needn't handle non-finite values.
Results may differ from a plain program's by a relative error of at most 0.0058.
Values may be sent and summed in bfloat16 or wider, within the bound.
A program may use at most 128 MiB of HBM per device.

v0:
```python
import jax
import jax.numpy as jnp
from jax import lax
from jax.sharding import PartitionSpec as P

eps = 1e-05


def slot_rank(owner, groups):
    marks = (owner[:, None] == jnp.arange(groups, dtype=jnp.int32)[None, :]).astype(jnp.int32)
    before = jnp.cumsum(marks, axis=0) - marks
    return jnp.sum(before * marks, axis=1)


def on_device(
    hash_tables, byte_table, byte_ids, hash_owner, hash_offset, gain, proj_weight, cotangent
):
    groups = lax.axis_size("table")
    half = lax.axis_index("mp")
    ngram = hash_tables.shape[0]
    rows_dev = hash_tables.shape[1]
    width = hash_tables.shape[2]
    tokens = byte_ids.shape[0]
    full_width = gain.shape[0]
    capacity = 2 * tokens // groups
    slots = []
    requests = []
    for k in range(ngram):
        owner = hash_owner[k, :, 0]
        slot = owner * capacity + slot_rank(owner, groups)
        slots.append(slot)
        wanted = jnp.zeros((groups * capacity,), jnp.int32).at[slot].set(hash_offset[k])
        requests.append(wanted.reshape(groups, capacity))
    codes = jnp.arange(byte_table.shape[0], dtype=jnp.int32)
    picks = (byte_ids[:, None] == codes[None, :]).astype(jnp.bfloat16)
    summed = jnp.dot(picks, byte_table, preferred_element_type=jnp.float32)
    incoming = []
    stacked = jnp.stack(requests, axis=1)
    asked = lax.all_to_all(stacked, "table", split_axis=0, concat_axis=0, tiled=True)
    which = jnp.arange(ngram, dtype=jnp.int32)[None, :, None]
    looked = hash_tables[which, asked]
    fetched = lax.all_to_all(looked, "table", split_axis=0, concat_axis=0, tiled=True)
    for k in range(ngram):
        summed = summed + fetched[:, k].reshape(-1, width)[slots[k]].astype(jnp.float32)
        incoming.append(asked[:, k])
    embedded = summed.astype(jnp.bfloat16)
    values = embedded.astype(jnp.float32)
    gain_half = lax.dynamic_slice_in_dim(gain, half * width, width)
    total = lax.psum(jnp.sum(values * values, axis=1), "mp")
    scale = lax.rsqrt(total / full_width + eps)[:, None]
    normed_half = (values * scale * gain_half[None, :]).astype(jnp.bfloat16)
    normed = lax.all_gather(normed_half, "mp", axis=1, tiled=True)
    weight = lax.all_gather(proj_weight, "table", axis=0, tiled=True)
    projected = jnp.dot(normed, weight, preferred_element_type=jnp.float32).astype(jnp.bfloat16)
    partial_grad = lax.dot_general(
        cotangent, weight, (((1,), (1,)), ((), ())), preferred_element_type=jnp.float32
    )
    dnormed = lax.psum_scatter(partial_grad, "mp", scatter_dimension=1, tiled=True)
    scaled = dnormed * gain_half[None, :]
    inner = lax.psum(jnp.sum(values * scaled, axis=1), "mp")[:, None] / full_width
    dembed = (scale * scaled - values * scale * scale * scale * inner).astype(jnp.bfloat16)
    sends = []
    for k in range(ngram):
        outgoing = jnp.zeros((groups * capacity, width), jnp.bfloat16).at[slots[k]].set(dembed)
        sends.append(outgoing.reshape(groups, capacity, width))
    grads = []
    arrived = lax.all_to_all(
        jnp.stack(sends, axis=1), "table", split_axis=0, concat_axis=0, tiled=True
    )
    for k in range(ngram):
        total = (
            jnp.zeros((rows_dev, width), jnp.float32)
            .at[incoming[k].reshape(-1)]
            .add(arrived[:, k].reshape(-1, width).astype(jnp.float32))
        )
        grads.append(total.astype(jnp.bfloat16))
    return (projected, jnp.stack(grads))


def solution(mesh):
    return jax.shard_map(
        on_device,
        mesh=mesh,
        in_specs=(
            P(None, "table", "mp"),
            P(None, "mp"),
            P("table"),
            P(None, "table", None),
            P(None, "table"),
            P(),
            P("table", "mp"),
            P("table", "mp"),
        ),
        out_specs=(P("table", "mp"), P(None, "table", "mp")),
        check_vma=False,
    )
```

profile of v0, /device:TPU:14, one launch (start us, length us, event | category | flops | bytes accessed | tf_op | source)
XLA Modules:
  0.0 479.1 jit_solution(1492231319341505479)
XLA Ops:
  14.9 11.2 %all_to_all.15 = s32[16,2,32]{2,1,0:T(2,128)S(1)} all-to-all(s32[16,2,32]{2,1,0:T(2,128)S(1)} %pad_add_fusion), channel_id=1, replica_groups=mesh['table'=16,'mp'=2] {'table'}, dimensions={0} | all-to-all | bytes 8192 | tf_op jit(solution)/shard_map/all_to_all | solution.py:39
  26.2 25.9 %gather_fusion = bf16[1024,2048]{1,0:T(8,128)(2,1)} fusion(bf16[2,1024,2048]{2,1,0:T(8,128)(2,1)} %param.8, s32[1024]{0:T(1024)S(1)} %reshape.166), kind=kCustom, calls=%fused_computation | custom fusion | bytes 8396800 | tf_op jit(solution)/shard_map/gather | solution.py:41
  52.1 14.9 %all-to-all-start.1 = ((bf16[16,2,32,2048]{3,2,1,0:T(8,128)(2,1)}), bf16[16,2,32,2048]{3,2,1,0:T(8,128)(2,1)}, u32[]{:S(2)}, u32[]{:S(2)}) async-start(bf16[16,2,32,2048]{3,2,1,0:T(8,128)(2,1)} %bitcast.88), calls=%async_computation.1 | async-start | bytes 8388608 | tf_op jit(solution)/shard_map/all_to_all | solution.py:42
  67.1 211.2 %all-gather.5.cloned.1.call-done = bf16[4096,2048]{1,0:T(8,128)(2,1)} async-done(((bf16[256,2048]{1,0:T(8,128)(2,1)}), bf16[4096,2048]{1,0:T(8,128)(2,1)}) %all-gather.5.cloned.1.call-update) | async-done | bytes 16777232 | tf_op jit(solution)/shard_map/all_gather | solution.py:53
  278.3 10.2 %fusion.42 = f32[256,4096]{1,0:T(8,128)} fusion(bf16[256,2048]{1,0:T(8,128)(2,1)S(1)} %copy-done, bf16[4096,2048]{1,0:T(8,128)(2,1)} %all-gather.5.cloned.1.call-done), kind=kOutput, calls=%fused_computation.85 | convolution fusion | flops 4294967296 | bytes 22020096 | tf_op jit(solution)/shard_map/dot_general | solution.py:55
  289.2 4.0 fusion.39
  293.2 5.2 %gather_fusion.1 = bf16[256,2048]{1,0:T(8,128)(2,1)} fusion(bf16[512,2048]{1,0:T(8,128)(2,1)} %bitcast.87, s32[1024]{0:T(1024)S(1)} %pad_clamp_fusion.1), kind=kCustom, calls=%fused_computation.1 | custom fusion | bytes 2098176 | tf_op jit(solution)/shard_map/gather | solution.py:44
  298.5 2.3 gather_fusion.2
  300.8 2.6 reduce-scatter.2.cloned.1.call-done
  303.4 3.6 fusion.16
  307.1 2.6 all-reduce
  311.8 3.5 scatter_custom_fusion.3
  315.3 4.4 scatter_custom_fusion.2
  319.8 4.0 pad_maximum_fusion.1
  323.7 6.9 %all-to-all-start.2 = ((bf16[16,2,32,2048]{3,2,1,0:T(8,128)(2,1)}), bf16[16,2,32,2048]{3,2,1,0:T(8,128)(2,1)}, u32[]{:S(2)}, u32[]{:S(2)}) async-start(bf16[16,2,32,2048]{3,2,1,0:T(8,128)(2,1)} %pad_maximum_fusion.1), calls=%async_computation.3 | async-start | bytes 8388608 | tf_op jit(solution)/shard_map/all_to_all | solution.py:67
  331.6 13.1 %all-gather.3.cloned.1.call-done = bf16[256,4096]{1,0:T(8,128)(2,1)} async-done(((bf16[256,2048]{1,0:T(8,128)(2,1)}), bf16[256,4096]{1,0:T(8,128)(2,1)}) %all-gather.3.cloned.1.call-update) | async-done | bytes 2097168 | tf_op jit(solution)/shard_map/all_gather | solution.py:52
  344.8 11.9 %convolution_convert_fusion = bf16[256,2048]{1,0:T(8,128)(2,1)} fusion(bf16[256,4096]{1,0:T(8,128)(2,1)} %all-gather.3.cloned.1.call-done, bf16[4096,2048]{1,0:T(8,128)(2,1)} %all-gather.5.cloned.1.call-done), kind=kOutput, calls=%fused_computation.25 | convolution fusion | flops 4295491584 | bytes 19922944 | tf_op jit(solution)/shard_map/dot_general | solution.py:54
  356.6 69.6 %all-to-all-done.2 = bf16[16,2,32,2048]{3,2,1,0:T(8,128)(2,1)} async-done(((bf16[16,2,32,2048]{3,2,1,0:T(8,128)(2,1)}), bf16[16,2,32,2048]{3,2,1,0:T(8,128)(2,1)}, u32[]{:S(2)}, u32[]{:S(2)}) %all-to-all-start.2) | async-done | bytes 4194336 | tf_op jit(solution)/shard_map/all_to_all | solution.py:67
  426.3 4.0 fusion.38
  430.3 12.2 %scatter_custom_fusion.5 = f32[1024,2048]{1,0:T(8,128)} fusion(s32[512]{0:T(512)S(1)} %bitcast.106, bf16[512,2048]{1,0:T(8,128)(2,1)} %bitcast.92, f32[]{:T(128)} %constant.15.clone.1), kind=kCustom, calls=%fused_computation.11 | custom fusion | flops 2097152 | bytes 10485764 | tf_op jit(solution)/shard_map/scatter-add | solution.py:74
  442.5 6.0 %convert_bitcast_fusion = bf16[1,1024,2048]{2,1,0:T(8,128)(2,1)} fusion(f32[1024,2048]{1,0:T(8,128)} %scatter_custom_fusion.5), kind=kLoop, calls=%fused_computation.15 | loop fusion | flops 2097152 | bytes 12582912 | tf_op jit(solution)/shard_map/stack | solution.py:77
  448.5 11.0 %scatter_custom_fusion.4 = f32[1024,2048]{1,0:T(8,128)} fusion(s32[512]{0:T(512)S(1)} %bitcast.105, bf16[512,2048]{1,0:T(8,128)(2,1)S(1)} %bitcast.91, f32[]{:T(128)} %constant.15.clone.1), kind=kCustom, calls=%fused_computation.13 | custom fusion | flops 2097152 | bytes 10485764 | tf_op jit(solution)/shard_map/scatter-add | solution.py:74
  459.5 6.2 %convert_bitcast_fusion.1 = bf16[1,1024,2048]{2,1,0:T(8,128)(2,1)} fusion(f32[1024,2048]{1,0:T(8,128)} %scatter_custom_fusion.4), kind=kLoop, calls=%fused_computation.16 | loop fusion | flops 2097152 | bytes 12582912 | tf_op jit(solution)/shard_map/stack | solution.py:77
  465.6 6.4 %pad_maximum_fusion = bf16[2,1024,2048]{2,1,0:T(8,128)(2,1)} fusion(bf16[1,1024,2048]{2,1,0:T(8,128)(2,1)S(1)} %copy-done.2, bf16[1,1024,2048]{2,1,0:T(8,128)(2,1)} %convert_bitcast_fusion.1), kind=kLoop, calls=%fused_computation.9 | loop fusion | flops 4194304 | bytes 16777216 | tf_op jit(solution)/shard_map/stack | solution.py:77
  (52 shorter events, 11.6 us)
Async XLA Ops:
  7.2 271.2 %copy-start = (bf16[256,2048]{1,0:T(8,128)(2,1)S(1)}, bf16[256,2048]{1,0:T(8,128)(2,1)}, u32[]{:S(2)}) copy-start(bf16[256,2048]{1,0:T(8,128)(2,1)} %param.15) | copy-start | bytes 3145732
  7.2 271.1 %all-gather.5.cloned.1.call-start = ((), (), s32[]{:S(2)}) async-start(), calls=%async_computation.5 | async-start | bytes 17825792 | tf_op jit(solution)/shard_map/all_gather | solution.py:53
  52.1 237.1 %all-to-all-start.1 = ((bf16[16,2,32,2048]{3,2,1,0:T(8,128)(2,1)}), bf16[16,2,32,2048]{3,2,1,0:T(8,128)(2,1)}, u32[]{:S(2)}, u32[]{:S(2)}) async-start(bf16[16,2,32,2048]{3,2,1,0:T(8,128)(2,1)} %bitcast.88), calls=%async_computation.1 | async-start | bytes 8388608 | tf_op jit(solution)/shard_map/all_to_all | solution.py:42
  67.0 236.4 %reduce-scatter.2.cloned.1.call-start = ((), (), s32[]{:S(2)}) async-start(), calls=%async_computation.6 | async-start | bytes 6291456 | tf_op jit(solution)/shard_map/reduce_scatter | solution.py:58
  288.5 0.7 copy-start.4
  298.5 5.0 %copy-start.5 = (s32[256]{0:T(256)S(1)}, s32[256]{0:T(256)}, u32[]{:S(2)}) copy-start(s32[256]{0:T(256)} %param.10) | copy-start | bytes 3076
  303.4 6.3 %copy-start.3 = (f32[256,2048]{1,0:T(8,128)S(1)}, f32[256,2048]{1,0:T(8,128)}, u32[]{:S(2)}) copy-start(f32[256,2048]{1,0:T(8,128)} %reduce-scatter.2.cloned.1.call-done) | copy-start | bytes 6291460
  323.7 102.5 %all-to-all-start.2 = ((bf16[16,2,32,2048]{3,2,1,0:T(8,128)(2,1)}), bf16[16,2,32,2048]{3,2,1,0:T(8,128)(2,1)}, u32[]{:S(2)}, u32[]{:S(2)}) async-start(bf16[16,2,32,2048]{3,2,1,0:T(8,128)(2,1)} %pad_maximum_fusion.1), calls=%async_computation.3 | async-start | bytes 8388608 | tf_op jit(solution)/shard_map/all_to_all | solution.py:67
  330.7 14.1 %all-gather.3.cloned.1.call-start = ((), (), s32[]{:S(2)}) async-start(), calls=%async_computation.4 | async-start | bytes 3145728 | tf_op jit(solution)/shard_map/all_gather | solution.py:52
  459.5 6.2 %copy-start.2 = (bf16[1,1024,2048]{2,1,0:T(8,128)(2,1)S(1)}, bf16[1,1024,2048]{2,1,0:T(8,128)(2,1)}, u32[]{:S(2)}) copy-start(bf16[1,1024,2048]{2,1,0:T(8,128)(2,1)} %convert_bitcast_fusion) | copy-start | bytes 12582916
  465.6 6.4 %copy-start.1 = (bf16[256,2048]{1,0:T(8,128)(2,1)S(1)}, bf16[256,2048]{1,0:T(8,128)(2,1)}, u32[]{:S(2)}) copy-start(bf16[256,2048]{1,0:T(8,128)(2,1)} %param.15) | copy-start | bytes 3145732
Sparse Core Ops, SparseCore 0:
  10.8 267.5 all-gather.4
  288.6 14.7 reduce-scatter.1
  333.0 11.6 all-gather.2
where the time goes:
time: 489 us; the launch traced here: 479 us
  waiting for transfers between devices  298 us (61%)
  local copies, waits for them, and re-layouts  55.3 us (11%)
  other arithmetic  50 us (10%)
  matrix products  25.6 us (5%)
  starting transfers between devices  22.2 us (5%)
  between operations  14.3 us (3%)
  blocking collectives  13.9 us (3%)
    all_gather x1, waiting for transfers between devices, on_device(): weight = lax.all_gather(proj_weight, 'table', axis=0, tiled=True)  211 us
    all_to_all x1, waiting for transfers between devices, on_device(): lax.all_to_all(jnp.stack(sends, axis=1), 'table', split_axis=0, concat_ax...  69.6 us
    gather x1, local copies, waits for them, and re-layouts, on_device(): looked = hash_tables[which, asked]  25.9 us
    scatter-add x2, other arithmetic, on_device(): total = jnp.zeros((rows_dev, width), jnp.float32).at[incoming[k].reshape(...  23.2 us
    another operation x3, other arithmetic, on_device(): return (projected, jnp.stack(grads))  18.6 us
    all_to_all x1, starting transfers between devices, on_device(): lax.all_to_all(looked, 'table', split_axis=0, concat_axis=0, tiled=True)  14.9 us
    all_gather x1, waiting for transfers between devices, on_device(): normed = lax.all_gather(normed_half, 'mp', axis=1, tiled=True)  13.1 us
    dot_general x1, matrix products, on_device(): jnp.dot(normed, weight, preferred_element_type=jnp.float32)  11.9 us
  transfers between devices with their start and end apart: 5, of which 4 were waited for; matrix products, arithmetic and copies ran while one was open for 14% of the time, Pallas kernels for 0%

commit v1 on v0

v1 whole, which is shorter than its diff:
```python
import functools

import jax
import jax.numpy as jnp
from jax import lax
from jax.experimental import pallas as pl
from jax.experimental.pallas import tpu as pltpu
from jax.sharding import PartitionSpec as P

eps = 1e-05
MESH = pl.DeviceIdType.MESH
ANY = pl.BlockSpec(memory_space=pl.ANY)


def slot_rank(owner, groups):
    marks = (owner[:, None] == jnp.arange(groups, dtype=jnp.int32)[None, :]).astype(jnp.int32)
    before = jnp.cumsum(marks, axis=0) - marks
    return jnp.sum(before * marks, axis=1)


def greet_table(n):
    me = lax.axis_index("table")
    barrier = pltpu.get_barrier_semaphore()
    for j in range(1, n):
        pl.semaphore_signal(
            barrier, inc=1, device_id={"table": lax.rem(me + j, n)}, device_id_type=MESH
        )
    pl.semaphore_wait(barrier, n - 1)


def start_exchange(n, src, dst, send, recv, window):
    me = lax.axis_index("table")
    copies = []
    for j in range(1, n):
        to = lax.rem(me + j, n)
        copy = pltpu.make_async_remote_copy(
            src_ref=window(src, to),
            dst_ref=window(dst, me),
            send_sem=send.at[j],
            recv_sem=recv.at[j],
            device_id={"table": to},
            device_id_type=MESH,
        )
        copy.start()
        copies.append(copy)
    return copies


def own_block(src, dst, hold, sem, window):
    me = lax.axis_index("table")
    load = pltpu.make_async_copy(window(src, me), hold, sem.at[0])
    load.start()
    load.wait()
    store = pltpu.make_async_copy(hold, window(dst, me), sem.at[1])
    store.start()
    return store


def first_window(ref, d):
    return ref.at[d]


def second_window(ref, d):
    return ref.at[:, d]


def exchange_kernel(n, window, x_ref, y_ref, hold, send, recv, local):
    greet_table(n)
    copies = start_exchange(n, x_ref, y_ref, send, recv, window)
    store = own_block(x_ref, y_ref, hold, local, window)
    store.wait()
    for copy in copies:
        copy.wait()


def exchange(x, n, window, collective_id):
    block = x.shape[1:] if window is first_window else x.shape[:1] + x.shape[2:]
    return pl.pallas_call(
        functools.partial(exchange_kernel, n, window),
        out_shape=jax.ShapeDtypeStruct(x.shape, x.dtype),
        in_specs=[ANY],
        out_specs=ANY,
        scratch_shapes=[
            pltpu.VMEM(block, x.dtype),
            pltpu.SemaphoreType.DMA((n,)),
            pltpu.SemaphoreType.DMA((n,)),
            pltpu.SemaphoreType.DMA((2,)),
        ],
        compiler_params=pltpu.CompilerParams(
            collective_id=collective_id, has_side_effects=True
        ),
    )(x)


def factors(n):
    major = 1
    while major * major < n:
        major *= 2
    return major, n // major


def snake(i):
    return (i // 2) * 2 + (i % 2 + i // 2) % 2


def gather_steps(n):
    major, minor = factors(n)
    total = 0
    for first, second in ((major, minor), (minor, major)):
        total += 2 * (first // 2) + first * 2 * (second // 2)
    return total


def start_gather(n, w_ref, out_ref, send, recv):
    major, minor = factors(n)
    me = lax.axis_index("table")
    row, place = me // minor, snake(me % minor)
    depth = w_ref.shape[0]
    half = depth // 2
    spot = [0]
    started = []

    def device(r, p):
        return lax.rem(r + major, major) * minor + snake(lax.rem(p + minor, minor))

    def send_block(origin, own, part, piece, to):
        size = half if piece is None else half // 2
        offset = part * half + (0 if piece is None else piece * size)
        at = pl.ds(pl.multiple_of(origin * depth + offset, size), size)
        src = w_ref.at[pl.ds(offset, size)] if own else out_ref.at[at]
        copy = pltpu.make_async_remote_copy(
            src_ref=src,
            dst_ref=out_ref.at[at],
            send_sem=send.at[spot[0]],
            recv_sem=recv.at[spot[0]],
            device_id={"table": to},
            device_id_type=MESH,
        )
        spot[0] += 1
        copy.start()
        started.append(copy)
        return copy

    class Chain:
        def __init__(self, part, ring, other, own):
            self.part, self.ring, self.other, self.own = part, ring, other, own
            self.size = major if ring == 0 else minor
            self.step = 0
            self.flight = None

        def at(self, shift):
            if self.ring == 0:
                return device(row + shift, self.other)
            return device(self.other, place + shift)

        def to(self, shift):
            if self.ring == 0:
                return device(row + shift, place)
            return device(row, place + shift)

        def go(self):
            last = self.step + 1 == self.size // 2
            pieces = (0, 1) if last else (None, None)
            own = self.own and self.step == 0
            self.flight = (
                send_block(self.at(-self.step), own, self.part, pieces[0], self.to(1)),
                send_block(self.at(self.step), own, self.part, pieces[1], self.to(-1)),
            )
            self.step += 1

        def arrive(self):
            for copy in self.flight:
                copy.wait_recv()
            if self.step < self.size // 2:
                self.go()

    firsts = [Chain(0, 0, place, True), Chain(1, 1, row, True)]
    seconds = [[Chain(0, 1, row, True)], [Chain(1, 0, place, True)]]
    for part in (0, 1):
        firsts[part].go()
    for part in (0, 1):
        seconds[part][0].go()
    for step in range(1, max(major, minor) // 2 + 1):
        for part in (0, 1):
            ring = (major, minor)[part]
            if step > ring // 2:
                continue
            firsts[part].arrive()
            shifts = (-step, step) if step < ring // 2 else (step,)
            for shift in shifts:
                if part == 0:
                    chain = Chain(0, 1, lax.rem(row + shift + major, major), False)
                else:
                    chain = Chain(1, 0, lax.rem(place + shift + minor, minor), False)
                chain.go()
                seconds[part].append(chain)
    for step in range(1, max(major, minor) // 2 + 1):
        for pair in zip(*seconds) if major == minor else [c for c in seconds]:
            for chain in pair:
                if step <= chain.size // 2:
                    chain.arrive()
    return started


def gather_kernel(n, w_ref, x_ref, w_out, y_ref, hold_w, hold_x, ws, wr, xs, xr, local):
    greet_table(n)
    copies = start_exchange(n, x_ref, y_ref, xs, xr, second_window)
    store = own_block(x_ref, y_ref, hold_x, local, second_window)
    me = lax.axis_index("table")
    depth = w_ref.shape[0]
    load = pltpu.make_async_copy(w_ref, hold_w, local.at[2])
    load.start()
    started = start_gather(n, w_ref, w_out, ws, wr)
    load.wait()
    put = pltpu.make_async_copy(
        hold_w, w_out.at[pl.ds(pl.multiple_of(me * depth, depth), depth)], local.at[3]
    )
    put.start()
    store.wait()
    put.wait()
    for copy in copies:
        copy.wait()
    for copy in started:
        copy.wait_send()


def gather_and_exchange(w, x, n, collective_id):
    steps = gather_steps(n)
    return pl.pallas_call(
        functools.partial(gather_kernel, n),
        out_shape=(
            jax.ShapeDtypeStruct((n * w.shape[0], w.shape[1]), w.dtype),
            jax.ShapeDtypeStruct(x.shape, x.dtype),
        ),
        in_specs=[ANY, ANY],
        out_specs=(ANY, ANY),
        scratch_shapes=[
            pltpu.VMEM(w.shape, w.dtype),
            pltpu.VMEM(x.shape[:1] + x.shape[2:], x.dtype),
            pltpu.SemaphoreType.DMA((steps,)),
            pltpu.SemaphoreType.DMA((steps,)),
            pltpu.SemaphoreType.DMA((n,)),
            pltpu.SemaphoreType.DMA((n,)),
            pltpu.SemaphoreType.DMA((4,)),
        ],
        compiler_params=pltpu.CompilerParams(
            collective_id=collective_id, has_side_effects=True
        ),
    )(w, x)


def greet_pair():
    other = 1 - lax.axis_index("mp")
    barrier = pltpu.get_barrier_semaphore()
    pl.semaphore_signal(barrier, inc=1, device_id={"mp": other}, device_id_type=MESH)
    pl.semaphore_wait(barrier, 1)
    return other


def join_kernel(x_ref, full_ref, send, recv, local):
    other = greet_pair()
    width = x_ref.shape[1]
    window = full_ref.at[:, pl.ds(pl.multiple_of((1 - other) * width, width), width)]
    copy = pltpu.make_async_remote_copy(
        src_ref=x_ref,
        dst_ref=window,
        send_sem=send,
        recv_sem=recv,
        device_id={"mp": other},
        device_id_type=MESH,
    )
    copy.start()
    keep = pltpu.make_async_copy(x_ref, window, local)
    keep.start()
    keep.wait()
    copy.wait()


def join_halves(x, collective_id):
    return pl.pallas_call(
        join_kernel,
        out_shape=jax.ShapeDtypeStruct((x.shape[0], 2 * x.shape[1]), x.dtype),
        in_specs=[pl.BlockSpec(memory_space=pltpu.VMEM)],
        out_specs=ANY,
        scratch_shapes=[pltpu.SemaphoreType.DMA] * 3,
        compiler_params=pltpu.CompilerParams(
            collective_id=collective_id, has_side_effects=True
        ),
    )(x)


def swap_kernel(part_ref, side_ref, part_out, side_out, send, recv):
    other = greet_pair()
    width = part_out.shape[1]
    copies = []
    pairs = (
        (part_ref.at[:, pl.ds(pl.multiple_of(other * width, width), width)], part_out),
        (side_ref, side_out),
    )
    for i, (src, dst) in enumerate(pairs):
        copy = pltpu.make_async_remote_copy(
            src_ref=src,
            dst_ref=dst,
            send_sem=send.at[i],
            recv_sem=recv.at[i],
            device_id={"mp": other},
            device_id_type=MESH,
        )
        copy.start()
        copies.append(copy)
    for copy in copies:
        copy.wait()


def swap_halves(part, side, collective_id):
    return pl.pallas_call(
        swap_kernel,
        out_shape=(
            jax.ShapeDtypeStruct((part.shape[0], part.shape[1] // 2), part.dtype),
            jax.ShapeDtypeStruct(side.shape, side.dtype),
        ),
        in_specs=[ANY, ANY],
        out_specs=(ANY, ANY),
        scratch_shapes=[pltpu.SemaphoreType.DMA((2,)), pltpu.SemaphoreType.DMA((2,))],
        compiler_params=pltpu.CompilerParams(
            collective_id=collective_id, has_side_effects=True
        ),
    )(part, side)


def on_device(
    hash_tables, byte_table, byte_ids, hash_owner, hash_offset, gain, proj_weight, cotangent
):
    groups = lax.axis_size("table")
    half = lax.axis_index("mp")
    ngram, rows_dev, width = hash_tables.shape
    tokens = byte_ids.shape[0]
    full_width = gain.shape[0]
    capacity = 2 * tokens // groups
    span = groups * capacity
    places = jnp.arange(span, dtype=jnp.int32)
    marks = []
    requests = []
    for k in range(ngram):
        owner = hash_owner[k, :, 0]
        slot = owner * capacity + slot_rank(owner, groups)
        mark = slot[:, None] == places[None, :]
        marks.append(mark)
        wanted = jnp.sum(jnp.where(mark, hash_offset[k][:, None] + 1, 0), axis=0) - 1
        requests.append(wanted.reshape(groups, capacity))
    stacked = jnp.stack(requests, axis=1)
    lanes = -(-capacity // 128) * 128
    levels = -(-ngram // 8) * 8
    stacked = jnp.pad(stacked, ((0, 0), (0, levels - ngram), (0, lanes - capacity)))
    asked = exchange(stacked, groups, first_window, 0)[:, :ngram, :capacity]
    asked = jnp.transpose(asked, (1, 0, 2)).reshape(ngram, span)
    rows = jnp.arange(rows_dev, dtype=jnp.int32)
    hits = (asked[:, :, None] == rows[None, None, :]).astype(jnp.bfloat16)
    looked = lax.dot_general(
        hits, hash_tables, (((2,), (1,)), ((0,), (0,))), preferred_element_type=jnp.float32
    ).astype(jnp.bfloat16)
    weight, fetched = gather_and_exchange(
        proj_weight, looked.reshape(ngram, groups, capacity, width), groups, 1
    )

    mark = jnp.concatenate(marks, axis=1).astype(jnp.bfloat16)
    codes = jnp.arange(byte_table.shape[0], dtype=jnp.int32)
    picks = (byte_ids[:, None] == codes[None, :]).astype(jnp.bfloat16)
    summed = jnp.dot(picks, byte_table, preferred_element_type=jnp.float32)
    summed = summed + jnp.dot(
        mark, fetched.reshape(ngram * span, width), preferred_element_type=jnp.float32
    )
    embedded_half = summed.astype(jnp.bfloat16)
    embedded = join_halves(embedded_half, 2)
    full = embedded.astype(jnp.float32)
    total = jnp.sum(full * full, axis=1)
    scale = lax.rsqrt(total / full_width + eps)[:, None]
    normed = (full * scale * gain[None, :]).astype(jnp.bfloat16)
    partial_grad = lax.dot_general(
        cotangent, weight, (((1,), (1,)), ((), ())), preferred_element_type=jnp.float32
    )
    inner_part = jnp.sum(full * (partial_grad * gain[None, :]), axis=1, keepdims=True)
    other_grad, other_inner = swap_halves(
        partial_grad, jnp.broadcast_to(inner_part, (tokens, 128)), 3
    )
    values = embedded_half.astype(jnp.float32)
    gain_half = lax.dynamic_slice_in_dim(gain, half * width, width)
    own_grad = lax.dynamic_slice_in_dim(partial_grad, half * width, width, axis=1)
    scaled = (own_grad + other_grad) * gain_half[None, :]
    inner = (inner_part + other_inner[:, :1]) / full_width
    dembed = (scale * scaled - values * scale * scale * scale * inner).astype(jnp.bfloat16)
    outgoing = lax.dot_general(
        mark, dembed, (((0,), (0,)), ((), ())), preferred_element_type=jnp.float32
    ).astype(jnp.bfloat16)
    arrived = exchange(
        outgoing.reshape(ngram, groups, capacity, width), groups, second_window, 4
    )
    grads = lax.dot_general(
        hits,
        arrived.reshape(ngram, span, width),
        (((1,), (1,)), ((0,), (0,))),
        preferred_element_type=jnp.float32,
    ).astype(jnp.bfloat16)
    projected = jnp.dot(normed, weight, preferred_element_type=jnp.float32).astype(jnp.bfloat16)
    return (projected, grads)


def solution(mesh):
    return jax.shard_map(
        on_device,
        mesh=mesh,
        in_specs=(
            P(None, "table", "mp"),
            P(None, "mp"),
            P("table"),
            P(None, "table", None),
            P(None, "table"),
            P(),
            P("table", "mp"),
            P("table", "mp"),
        ),
        out_specs=(P("table", "mp"), P(None, "table", "mp")),
        check_vma=False,
    )
```

time: 489 us -> 470 us (0.961); the launches traced: 479 us -> 469 us
  Pallas kernels: 0 us -> 403 us
  waiting for transfers between devices: 298 us -> 0 us
  local copies, waits for them, and re-layouts: 55.3 us -> 3.74 us
  other arithmetic: 50 us -> 3.83 us
  matrix products: 25.6 us -> 57.5 us
  starting transfers between devices: 22.2 us -> 0 us
  blocking collectives: 13.9 us -> 0 us
  between operations: 14.3 us -> 0.83 us
    pallas_call x0 -> x5, Pallas kernels: none -> 403 us  [the longest x1 273 us: gather_and_exchange(): pl.pallas_call(functools.partial(gather_kernel, n), out_shape=(jax.ShapeD...]
    all_gather x2 -> x0, waiting for transfers between devices: 224 us -> none  [the longest x1 211 us: on_device(): weight = lax.all_gather(proj_weight, 'table', axis=0, tiled=True)]
    all_to_all x2 -> x0, waiting for transfers between devices: 69.6 us -> none  [the longest x1 69.6 us: on_device(): lax.all_to_all(jnp.stack(sends, axis=1), 'table', split_axis=0, concat_ax...]
    gather x3 -> x0, local copies, waits for them, and re-layouts: 33.5 us -> none  [the longest x1 25.9 us: on_device(): looked = hash_tables[which, asked]]
    dot_general x0 -> x4, matrix products: none -> 27.7 us  [the longest x1 9.48 us: on_device(): lax.dot_general(hits, hash_tables, (((2,), (1,)), ((0,), (0,))), preferre...]
    scatter-add x2 -> x0, other arithmetic: 23.2 us -> none  [on_device(): total = jnp.zeros((rows_dev, width), jnp.float32).at[incoming[k].reshape(...]
    another operation x8 -> x4, other arithmetic: 23.8 us -> 1.24 us  [the longest x3 18.6 us: on_device(): return (projected, jnp.stack(grads))]
    all_to_all x2 -> x0, starting transfers between devices: 21.8 us -> none  [the longest x1 14.9 us: on_device(): lax.all_to_all(looked, 'table', split_axis=0, concat_axis=0, tiled=True)]
  transfers between devices with their start and end apart: 5 -> 0, of which waited for: 4 -> 0; matrix products, arithmetic and copies ran while one was open for 14% -> 0% of each run, Pallas kernels for 0% -> 0%
where the time goes in v1:
time: 470 us; the launch traced here: 469 us
  Pallas kernels  403 us (86%)
  matrix products  57.5 us (12%)
    pallas_call x1, Pallas kernels, gather_and_exchange(): pl.pallas_call(functools.partial(gather_kernel, n), out_shape=(jax.ShapeD...  273 us
    pallas_call x2, Pallas kernels, exchange(): pl.pallas_call(functools.partial(exchange_kernel, n, window), out_shape=j...  122 us
    dot_general x1, matrix products, on_device(): lax.dot_general(cotangent, weight, (((1,), (1,)), ((), ())), preferred_el...  19 us
    dot_general x1, matrix products, on_device(): lax.dot_general(hits, hash_tables, (((2,), (1,)), ((0,), (0,))), preferre...  9.48 us

profile of v1, /device:TPU:14, one launch (start us, length us, event | category | flops | bytes accessed | tf_op | source)
XLA Modules:
  0.0 469.2 jit_solution(3919337406693467977)
XLA Ops:
  0.6 0.8 slice_add_fusion.1
  1.4 0.7 fusion.33
  2.1 0.6 reduce-window.16
  2.7 0.2 slice_reduce_fusion
  3.0 0.2 select_reduce_fusion
  3.3 0.6 reduce-window.14
  3.9 0.2 slice_reduce_fusion.1
  4.5 0.6 pad.4.x_ref
  5.2 8.2 %shard_map.95 = s32[16,8,128]{2,1,0:T(8,128)} custom-call(s32[16,8,128]{2,1,0:T(8,128)} %pad.4.x_ref), custom_call_target="tpu_custom_call" | custom-call | tf_op jit(solution)/shard_map/pallas_call | solution.py:78
  13.4 0.8 slice_bitcast_fusion
  14.3 9.5 %fusion.5 = bf16[2,512,2048]{2,1,0:T(8,128)(2,1)} fusion(bf16[2,1024,2048]{2,1,0:T(8,128)(2,1)} %param.8, s32[2,512]{1,0:T(2,128)S(1)} %eq.123), kind=kOutput, calls=%fused_computation.10 | convolution fusion | flops 4298113024 | bytes 12587008 | tf_op jit(solution)/shard_map/dot_general | solution.py:359
  23.8 272.7 %shard_map.96 = (bf16[4096,2048]{1,0:T(8,128)(2,1)}, bf16[2,16,32,2048]{3,2,1,0:T(8,128)(2,1)}) custom-call(bf16[256,2048]{1,0:T(8,128)(2,1)} %w_ref.1, bf16[2,16,32,2048]{3,2,1,0:T(8,128)(2,1)} %bitcast.73), custom_call_target="tpu_custom_call" | custom-call | tf_op jit(solution)/shard_map/pallas_call | solution.py:229
  296.6 0.2 iota_compare_fusion.5
  296.8 3.5 fusion.20
  300.3 1.5 fusion.6.x_ref
  301.8 4.0 shard_map.97
  305.9 19.0 %fusion.3 = (f32[256]{0:T(256)S(1)}, f32[256]{0:T(256)S(1)}, f32[4096,256]{0,1:T(8,128)}) fusion(bf16[256,4096]{1,0:T(8,128)(2,1)} %shard_map.97, f32[4096]{0:T(1024)S(1)} %copy-done.4, bf16[4096,2048]{1,0:T(8,128)(2,1)} %get-tuple-element.7, bf16[256,2048]{1,0:T(8,128)(2,1)S(1)} %copy-done), kind=kOutput, calls=%fused_computation.7 | convolution fusion | flops 4301258752 | bytes 24135680 | tf_op jit(solution)/shard_map/dot_general | solution.py:379
  325.0 9.3 %convolution_convert_fusion.2 = bf16[256,2048]{1,0:T(8,128)(2,1)} fusion(bf16[4096,2048]{1,0:T(8,128)(2,1)} %get-tuple-element.7, bf16[256,4096]{1,0:T(8,128)(2,1)S(1)} %copy-done.2, f32[4096]{0:T(1024)S(1)} %copy-done.4, f32[256]{0:T(256)S(1)} %add_rsqrt_fusion), kind=kOutput, calls=%fused_computation.13 | convolution fusion | flops 4299685888 | bytes 19940352 | tf_op jit(solution)/shard_map/dot_general | solution.py:404
  334.3 0.7 broadcast_in_dim.42.side_ref
  335.0 4.7 %shard_map.98 = (f32[256,2048]{1,0:T(8,128)}, f32[256,128]{1,0:T(8,128)}) custom-call(f32[256,4096]{1,0:T(8,128)} %bitcast.72, f32[256,128]{1,0:T(8,128)} %broadcast_in_dim.42.side_ref), custom_call_target="tpu_custom_call" | custom-call | tf_op jit(solution)/shard_map/pallas_call | solution.py:316
  339.9 1.0 multiply_reduce_fusion
  340.9 5.8 %convolution_convert_fusion.1 = bf16[1024,2048]{1,0:T(8,128)(2,1)} fusion(f32[256,2048]{1,0:T(8,128)} %get-tuple-element.8, bf16[256,2048]{1,0:T(8,128)(2,1)S(1)} %copy-done.1, f32[4096,256]{0,1:T(8,128)} %get-tuple-element.16, s32[]{:T(128)S(6)} %select_n.13, f32[256]{0:T(256)S(1)} %multiply_reduce_fusion, f32[2048]{0:T(1024)S(1)} %dynamic_slice.7, ...), kind=kOutput, calls=%fused_computation.11 | convolution fusion | flops 1081344000 | bytes 9709572 | tf_op jit(solution)/shard_map/dot_general | solution.py:392
  346.7 113.6 %shard_map.99 = bf16[2,16,32,2048]{3,2,1,0:T(8,128)(2,1)} custom-call(bf16[2,16,32,2048]{3,2,1,0:T(8,128)(2,1)} %bitcast.71), custom_call_target="tpu_custom_call" | custom-call | tf_op jit(solution)/shard_map/pallas_call | solution.py:78
  460.2 8.9 %convolution_convert_fusion = bf16[2,1024,2048]{2,1,0:T(8,128)(2,1)} fusion(bf16[2,512,2048]{2,1,0:T(8,128)(2,1)} %bitcast.74, s32[2,512]{1,0:T(2,128)S(1)} %eq.123), kind=kOutput, calls=%fused_computation.3 | convolution fusion | flops 4300210176 | bytes 12587008 | tf_op jit(solution)/shard_map/dot_general | solution.py:398
  (33 shorter events, 0.9 us)
Async XLA Ops:
  0.6 305.3 %copy-start = (bf16[256,2048]{1,0:T(8,128)(2,1)S(1)}, bf16[256,2048]{1,0:T(8,128)(2,1)}, u32[]{:S(2)}) copy-start(bf16[256,2048]{1,0:T(8,128)(2,1)} %param.15) | copy-start | bytes 3145732
  296.5 3.8 copy-start.3
  296.5 3.8 copy-start.5
  300.3 5.6 %copy-start.4 = (f32[4096]{0:T(1024)S(1)}, f32[4096]{0:T(1024)}, u32[]{:S(2)}) copy-start(f32[4096]{0:T(1024)} %param.13) | copy-start | bytes 49156
  305.9 19.0 %copy-start.2 = (bf16[256,4096]{1,0:T(8,128)(2,1)S(1)}, bf16[256,4096]{1,0:T(8,128)(2,1)}, u32[]{:S(2)}) copy-start(bf16[256,4096]{1,0:T(8,128)(2,1)} %shard_map.97) | copy-start | bytes 6291460
  334.2 6.7 %copy-start.1 = (bf16[256,2048]{1,0:T(8,128)(2,1)S(1)}, bf16[256,2048]{1,0:T(8,128)(2,1)}, u32[]{:S(2)}) copy-start(bf16[256,2048]{1,0:T(8,128)(2,1)} %fusion.6.x_ref) | copy-start | bytes 3145732

commit v2 on v1

--- a/solution.py
+++ b/solution.py
@@ -28,7 +28,7 @@
     pl.semaphore_wait(barrier, n - 1)
 
 
-def start_exchange(n, src, dst, send, recv, window):
+def exchange_copies(n, src, dst, send, recv, window):
     me = lax.axis_index("table")
     copies = []
     for j in range(1, n):
@@ -41,7 +41,6 @@
             device_id={"table": to},
             device_id_type=MESH,
         )
-        copy.start()
         copies.append(copy)
     return copies
 
@@ -66,7 +65,9 @@
 
 def exchange_kernel(n, window, x_ref, y_ref, hold, send, recv, local):
     greet_table(n)
-    copies = start_exchange(n, x_ref, y_ref, send, recv, window)
+    copies = exchange_copies(n, x_ref, y_ref, send, recv, window)
+    for copy in copies:
+        copy.start()
     store = own_block(x_ref, y_ref, hold, local, window)
     store.wait()
     for copy in copies:
@@ -105,31 +106,32 @@
 
 def gather_steps(n):
     major, minor = factors(n)
-    total = 0
-    for first, second in ((major, minor), (minor, major)):
-        total += 2 * (first // 2) + first * 2 * (second // 2)
-    return total
-
-
-def start_gather(n, w_ref, out_ref, send, recv):
+    return 2 * (major - 1) + (2 * major - 1) * 2 * (minor // 2)
+
+
+def start_gather(n, w_ref, out_ref, send, recv, between):
     major, minor = factors(n)
     me = lax.axis_index("table")
     row, place = me // minor, snake(me % minor)
     depth = w_ref.shape[0]
-    half = depth // 2
     spot = [0]
-    started = []
-
-    def device(r, p):
-        return lax.rem(r + major, major) * minor + snake(lax.rem(p + minor, minor))
-
-    def send_block(origin, own, part, piece, to):
-        size = half if piece is None else half // 2
-        offset = part * half + (0 if piece is None else piece * size)
+    sends = []
+
+    def always(body):
+        body()
+
+    def when(condition):
+        return always if condition is None else pl.when(condition)
+
+    def on_ring(r, shift):
+        return r * minor + snake(lax.rem(place + shift + minor, minor))
+
+    def copy_of(origin, own, piece, to):
+        size = depth if piece is None else depth // 2
+        offset = 0 if piece is None else piece * size
         at = pl.ds(pl.multiple_of(origin * depth + offset, size), size)
-        src = w_ref.at[pl.ds(offset, size)] if own else out_ref.at[at]
         copy = pltpu.make_async_remote_copy(
-            src_ref=src,
+            src_ref=w_ref.at[pl.ds(offset, size)] if own else out_ref.at[at],
             dst_ref=out_ref.at[at],
             send_sem=send.at[spot[0]],
             recv_sem=recv.at[spot[0]],
@@ -137,91 +139,89 @@
             device_id_type=MESH,
         )
         spot[0] += 1
-        copy.start()
-        started.append(copy)
         return copy
 
-    class Chain:
-        def __init__(self, part, ring, other, own):
-            self.part, self.ring, self.other, self.own = part, ring, other, own
-            self.size = major if ring == 0 else minor
-            self.step = 0
-            self.flight = None
-
-        def at(self, shift):
-            if self.ring == 0:
-                return device(row + shift, self.other)
-            return device(self.other, place + shift)
-
-        def to(self, shift):
-            if self.ring == 0:
-                return device(row + shift, place)
-            return device(row, place + shift)
-
-        def go(self):
-            last = self.step + 1 == self.size // 2
-            pieces = (0, 1) if last else (None, None)
-            own = self.own and self.step == 0
-            self.flight = (
-                send_block(self.at(-self.step), own, self.part, pieces[0], self.to(1)),
-                send_block(self.at(self.step), own, self.part, pieces[1], self.to(-1)),
-            )
-            self.step += 1
-
-        def arrive(self):
-            for copy in self.flight:
-                copy.wait_recv()
-            if self.step < self.size // 2:
-                self.go()
-
-    firsts = [Chain(0, 0, place, True), Chain(1, 1, row, True)]
-    seconds = [[Chain(0, 1, row, True)], [Chain(1, 0, place, True)]]
-    for part in (0, 1):
-        firsts[part].go()
-    for part in (0, 1):
-        seconds[part][0].go()
-    for step in range(1, max(major, minor) // 2 + 1):
-        for part in (0, 1):
-            ring = (major, minor)[part]
-            if step > ring // 2:
-                continue
-            firsts[part].arrive()
-            shifts = (-step, step) if step < ring // 2 else (step,)
-            for shift in shifts:
-                if part == 0:
-                    chain = Chain(0, 1, lax.rem(row + shift + major, major), False)
-                else:
-                    chain = Chain(1, 0, lax.rem(place + shift + minor, minor), False)
-                chain.go()
-                seconds[part].append(chain)
-    for step in range(1, max(major, minor) // 2 + 1):
-        for pair in zip(*seconds) if major == minor else [c for c in seconds]:
-            for chain in pair:
-                if step <= chain.size // 2:
-                    chain.arrive()
-    return started
+    def line_copy(step, way):
+        origin = lax.rem(row - way * (step - 1) + major, major)
+        to = lax.rem(row + way + major, major)
+        return copy_of(
+            origin * minor + me % minor, step == 1, None, to * minor + me % minor
+        )
+
+    def has(shift):
+        return jnp.logical_and(row + shift >= 0, row + shift < major)
+
+    def line_go(step):
+        copies = []
+        for way in (1, -1):
+            copy = line_copy(step, way)
+            leaves = jnp.logical_and(has(-way * (step - 1)), has(way))
+            pl.when(leaves)(copy.start)
+            sends.append((leaves, copy))
+            copies.append((has(-way * step), copy))
+        return copies
+
+    def ring_go(block, own, present, step):
+        pieces = (0, 1) if step == minor // 2 else (None, None)
+        first = own and step == 1
+        pair = (
+            copy_of(on_ring(block, 1 - step), first, pieces[0], on_ring(row, 1)),
+            copy_of(on_ring(block, step - 1), first, pieces[1], on_ring(row, -1)),
+        )
+        for copy in pair:
+            when(present)(copy.start)
+            sends.append((present, copy))
+        return pair
+
+    blocks = [(row, True, None)]
+    flight = line_go(1)
+    rings = [ring_go(row, True, None, 1)]
+    between(0)
+    for step in range(1, major):
+        for present, copy in flight:
+            pl.when(present)(copy.wait_recv)
+        if step + 1 < major:
+            flight = line_go(step + 1)
+        for way in (1, -1):
+            block = lax.rem(row - way * step + major, major)
+            blocks.append((block, False, has(-way * step)))
+            rings.append(ring_go(*blocks[-1], 1))
+        between(step)
+    for step in range(1, minor // 2 + 1):
+        for i, (block, own, present) in enumerate(blocks):
+            for copy in rings[i]:
+                when(present)(copy.wait_recv)
+            if step < minor // 2:
+                rings[i] = ring_go(block, own, present, step + 1)
+    return [(when(present), copy) for present, copy in sends]
 
 
 def gather_kernel(n, w_ref, x_ref, w_out, y_ref, hold_w, hold_x, ws, wr, xs, xr, local):
     greet_table(n)
-    copies = start_exchange(n, x_ref, y_ref, xs, xr, second_window)
-    store = own_block(x_ref, y_ref, hold_x, local, second_window)
     me = lax.axis_index("table")
     depth = w_ref.shape[0]
     load = pltpu.make_async_copy(w_ref, hold_w, local.at[2])
     load.start()
-    started = start_gather(n, w_ref, w_out, ws, wr)
+    copies = exchange_copies(n, x_ref, y_ref, xs, xr, second_window)
+    share = -(-(n - 1) // factors(n)[0])
+
+    def between(i):
+        for copy in copies[i * share : (i + 1) * share]:
+            copy.start()
+
+    started = start_gather(n, w_ref, w_out, ws, wr, between)
     load.wait()
     put = pltpu.make_async_copy(
         hold_w, w_out.at[pl.ds(pl.multiple_of(me * depth, depth), depth)], local.at[3]
     )
     put.start()
+    store = own_block(x_ref, y_ref, hold_x, local, second_window)
     store.wait()
     put.wait()
     for copy in copies:
         copy.wait()
-    for copy in started:
-        copy.wait_send()
+    for when, copy in started:
+        when(copy.wait_send)
 
 
 def gather_and_exchange(w, x, n, collective_id):
@@ -392,8 +392,12 @@
     outgoing = lax.dot_general(
         mark, dembed, (((0,), (0,)), ((), ())), preferred_element_type=jnp.float32
     ).astype(jnp.bfloat16)
-    arrived = exchange(
-        outgoing.reshape(ngram, groups, capacity, width), groups, second_window, 4
+    arrived = lax.all_to_all(
+        outgoing.reshape(ngram, groups, capacity, width),
+        "table",
+        split_axis=1,
+        concat_axis=1,
+        tiled=True,
     )
     grads = lax.dot_general(
         hits,

time: 470 us -> 419 us (0.89)
  Pallas kernels: 403 us -> 204 us
  waiting for transfers between devices: 0 us -> 86.2 us
  starting transfers between devices: 0 us -> 61.1 us
  local copies, waits for them, and re-layouts: 3.74 us -> 8.57 us
    pallas_call x2 -> x1, Pallas kernels: 122 us -> 8.21 us  [exchange(): pl.pallas_call(functools.partial(exchange_kernel, n, window), out_shape=j...]
    all_to_all x0 -> x1, waiting for transfers between devices: none -> 86.2 us  [on_device(): lax.all_to_all(outgoing.reshape(ngram, groups, capacity, width), 'table',...]
    pallas_call x1, Pallas kernels: 273 us -> 187 us  [gather_and_exchange(): pl.pallas_call(functools.partial(gather_kernel, n), out_shape=(jax.ShapeD...]
    all_to_all x0 -> x1, starting transfers between devices: none -> 61.1 us  [on_device(): lax.all_to_all(outgoing.reshape(ngram, groups, capacity, width), 'table',...]
  transfers between devices with their start and end apart: 0 -> 1, of which waited for: 0 -> 1; matrix products, arithmetic and copies ran while one was open for 0% -> 2% of each run, Pallas kernels for 0% -> 0%
where the time goes in v2:
time: 419 us; the launch traced here: 418 us
  Pallas kernels  204 us (49%)
  waiting for transfers between devices  86.2 us (21%)
  starting transfers between devices  61.1 us (15%)
  matrix products  53.3 us (13%)
  local copies, waits for them, and re-layouts  8.57 us (2%)
    pallas_call x1, Pallas kernels, gather_and_exchange(): pl.pallas_call(functools.partial(gather_kernel, n), out_shape=(jax.ShapeD...  187 us
    all_to_all x1, waiting for transfers between devices, on_device(): lax.all_to_all(outgoing.reshape(ngram, groups, capacity, width), 'table',...  86.2 us
    all_to_all x1, starting transfers between devices, on_device(): lax.all_to_all(outgoing.reshape(ngram, groups, capacity, width), 'table',...  61.1 us
    dot_general x1, matrix products, on_device(): lax.dot_general(cotangent, weight, (((1,), (1,)), ((), ())), preferred_el...  18.9 us
    dot_general x1, matrix products, on_device(): lax.dot_general(hits, hash_tables, (((2,), (1,)), ((0,), (0,))), preferre...  9.47 us
    dot_general x1, matrix products, on_device(): jnp.dot(normed, weight, preferred_element_type=jnp.float32)  9.3 us
  transfers between devices with their start and end apart: 1, of which 1 were waited for; matrix products, arithmetic and copies ran while one was open for 2% of the time, Pallas kernels for 0%

profile of v2, /device:TPU:14, one launch (start us, length us, event | category | flops | bytes accessed | tf_op | source)
XLA Modules:
  0.0 418.2 jit_solution(13040888867034256680)
XLA Ops:
  0.7 0.8 slice_add_fusion.1
  1.4 0.7 fusion.33
  2.1 0.6 reduce-window.16
  3.3 0.6 reduce-window.14
  4.2 0.2 iota_compare_fusion.5
  4.7 0.6 pad.4.x_ref
  5.4 8.2 %shard_map.95 = s32[16,8,128]{2,1,0:T(8,128)} custom-call(s32[16,8,128]{2,1,0:T(8,128)} %pad.4.x_ref), custom_call_target="tpu_custom_call" | custom-call | tf_op jit(solution)/shard_map/pallas_call | solution.py:79
  13.6 0.8 slice_bitcast_fusion
  14.5 9.5 %fusion.5 = bf16[2,512,2048]{2,1,0:T(8,128)(2,1)} fusion(bf16[2,1024,2048]{2,1,0:T(8,128)(2,1)} %param.8, s32[2,512]{1,0:T(2,128)S(1)} %eq.123), kind=kOutput, calls=%fused_computation.10 | convolution fusion | flops 4298113024 | bytes 12587008 | tf_op jit(solution)/shard_map/dot_general | solution.py:359
  24.0 187.4 %shard_map.96 = (bf16[4096,2048]{1,0:T(8,128)(2,1)}, bf16[2,16,32,2048]{3,2,1,0:T(8,128)(2,1)}) custom-call(bf16[256,2048]{1,0:T(8,128)(2,1)} %w_ref.1, bf16[2,16,32,2048]{3,2,1,0:T(8,128)(2,1)} %bitcast.73), custom_call_target="tpu_custom_call" | custom-call | tf_op jit(solution)/shard_map/pallas_call | solution.py:229
  211.5 3.5 fusion.20
  215.0 1.5 fusion.6.x_ref
  216.5 4.0 shard_map.97
  220.6 18.9 %fusion.3 = (f32[256]{0:T(256)S(1)}, f32[256]{0:T(256)S(1)}, f32[4096,256]{0,1:T(8,128)}) fusion(bf16[256,4096]{1,0:T(8,128)(2,1)} %shard_map.97, f32[4096]{0:T(1024)S(1)} %copy-done.5, bf16[4096,2048]{1,0:T(8,128)(2,1)} %get-tuple-element.7, bf16[256,2048]{1,0:T(8,128)(2,1)S(1)} %copy-done), kind=kOutput, calls=%fused_computation.7 | convolution fusion | flops 4301258752 | bytes 24135680 | tf_op jit(solution)/shard_map/dot_general | solution.py:379
  239.6 0.7 broadcast_in_dim.42.side_ref
  240.4 4.7 %shard_map.98 = (f32[256,2048]{1,0:T(8,128)}, f32[256,128]{1,0:T(8,128)}) custom-call(f32[256,4096]{1,0:T(8,128)} %bitcast.72, f32[256,128]{1,0:T(8,128)} %broadcast_in_dim.42.side_ref), custom_call_target="tpu_custom_call" | custom-call | tf_op jit(solution)/shard_map/pallas_call | solution.py:316
  245.1 1.0 multiply_reduce_fusion
  246.2 3.8 convolution_convert_fusion.1
  250.0 2.3 copy.36
  252.3 61.1 %all-to-all-start = ((bf16[2,16,32,2048]{3,2,0,1:T(8,128)(2,1)}), bf16[2,16,32,2048]{3,2,0,1:T(8,128)(2,1)}, u32[]{:S(2)}, u32[]{:S(2)}) async-start(bf16[2,16,32,2048]{3,2,0,1:T(8,128)(2,1)} %copy.36), calls=%async_computation | async-start | bytes 8388608 | tf_op jit(solution)/shard_map/all_to_all | solution.py:395
  313.4 9.3 %convolution_convert_fusion.2 = bf16[256,2048]{1,0:T(8,128)(2,1)} fusion(bf16[4096,2048]{1,0:T(8,128)(2,1)} %get-tuple-element.7, bf16[256,4096]{1,0:T(8,128)(2,1)S(1)} %copy-done.3, f32[4096]{0:T(1024)S(1)} %copy-done.5, f32[256]{0:T(256)S(1)} %add_rsqrt_fusion), kind=kOutput, calls=%fused_computation.13 | convolution fusion | flops 4299685888 | bytes 19940352 | tf_op jit(solution)/shard_map/dot_general | solution.py:408
  322.7 86.2 %all-to-all-done = bf16[2,16,32,2048]{3,2,0,1:T(8,128)(2,1)} async-done(((bf16[2,16,32,2048]{3,2,0,1:T(8,128)(2,1)}), bf16[2,16,32,2048]{3,2,0,1:T(8,128)(2,1)}, u32[]{:S(2)}, u32[]{:S(2)}) %all-to-all-start) | async-done | bytes 4194336 | tf_op jit(solution)/shard_map/all_to_all | solution.py:395
  409.0 2.5 copy.37
  411.5 6.8 %convolution_convert_fusion = bf16[2,1024,2048]{2,1,0:T(8,128)(2,1)} fusion(bf16[2,512,2048]{2,1,0:T(8,128)(2,1)S(1)} %bitcast.74, s32[2,512]{1,0:T(2,128)S(1)} %eq.123), kind=kOutput, calls=%fused_computation.3 | convolution fusion | flops 4300210176 | bytes 12587008 | tf_op jit(solution)/shard_map/dot_general | solution.py:402
  (39 shorter events, 1.5 us)
Async XLA Ops:
  0.6 219.9 %copy-start = (bf16[256,2048]{1,0:T(8,128)(2,1)S(1)}, bf16[256,2048]{1,0:T(8,128)(2,1)}, u32[]{:S(2)}) copy-start(bf16[256,2048]{1,0:T(8,128)(2,1)} %param.15) | copy-start | bytes 3145732
  211.4 3.6 copy-start.4
  211.4 3.6 copy-start.6
  215.0 5.5 %copy-start.5 = (f32[4096]{0:T(1024)S(1)}, f32[4096]{0:T(1024)}, u32[]{:S(2)}) copy-start(f32[4096]{0:T(1024)} %param.13) | copy-start | bytes 49156
  239.5 6.7 %copy-start.2 = (bf16[256,2048]{1,0:T(8,128)(2,1)S(1)}, bf16[256,2048]{1,0:T(8,128)(2,1)}, u32[]{:S(2)}) copy-start(bf16[256,2048]{1,0:T(8,128)(2,1)} %fusion.6.x_ref) | copy-start | bytes 3145732
  239.6 6.5 %dynamic-slice-start = ((f32[4096]{0:T(1024)}, s32[]{:T(128)}), f32[2048]{0:T(1024)S(1)}, s32[]{:S(2)}) async-start(f32[4096]{0:T(1024)} %param.13, s32[]{:T(128)} %select_n.13), calls=%async_computation.1 | async-start | bytes 16896 | tf_op jit(solution)/shard_map/dynamic_slice | solution.py:387
  252.3 61.1 %copy-start.3 = (bf16[256,4096]{1,0:T(8,128)(2,1)S(1)}, bf16[256,4096]{1,0:T(8,128)(2,1)}, u32[]{:S(2)}) copy-start(bf16[256,4096]{1,0:T(8,128)(2,1)} %shard_map.97) | copy-start | bytes 6291460
  252.3 156.6 %all-to-all-start = ((bf16[2,16,32,2048]{3,2,0,1:T(8,128)(2,1)}), bf16[2,16,32,2048]{3,2,0,1:T(8,128)(2,1)}, u32[]{:S(2)}, u32[]{:S(2)}) async-start(bf16[2,16,32,2048]{3,2,0,1:T(8,128)(2,1)} %copy.36), calls=%async_computation | async-start | bytes 8388608 | tf_op jit(solution)/shard_map/all_to_all | solution.py:395
  411.5 6.8 %copy-start.1 = (bf16[256,2048]{1,0:T(8,128)(2,1)S(1)}, bf16[256,2048]{1,0:T(8,128)(2,1)}, u32[]{:S(2)}) copy-start(bf16[256,2048]{1,0:T(8,128)(2,1)} %param.15) | copy-start | bytes 3145732

commit v3 on v2

--- a/solution.py
+++ b/solution.py
@@ -45,52 +45,8 @@
     return copies
 
 
-def own_block(src, dst, hold, sem, window):
-    me = lax.axis_index("table")
-    load = pltpu.make_async_copy(window(src, me), hold, sem.at[0])
-    load.start()
-    load.wait()
-    store = pltpu.make_async_copy(hold, window(dst, me), sem.at[1])
-    store.start()
-    return store
-
-
 def first_window(ref, d):
     return ref.at[d]
-
-
-def second_window(ref, d):
-    return ref.at[:, d]
-
-
-def exchange_kernel(n, window, x_ref, y_ref, hold, send, recv, local):
-    greet_table(n)
-    copies = exchange_copies(n, x_ref, y_ref, send, recv, window)
-    for copy in copies:
-        copy.start()
-    store = own_block(x_ref, y_ref, hold, local, window)
-    store.wait()
-    for copy in copies:
-        copy.wait()
-
-
-def exchange(x, n, window, collective_id):
-    block = x.shape[1:] if window is first_window else x.shape[:1] + x.shape[2:]
-    return pl.pallas_call(
-        functools.partial(exchange_kernel, n, window),
-        out_shape=jax.ShapeDtypeStruct(x.shape, x.dtype),
-        in_specs=[ANY],
-        out_specs=ANY,
-        scratch_shapes=[
-            pltpu.VMEM(block, x.dtype),
-            pltpu.SemaphoreType.DMA((n,)),
-            pltpu.SemaphoreType.DMA((n,)),
-            pltpu.SemaphoreType.DMA((2,)),
-        ],
-        compiler_params=pltpu.CompilerParams(
-            collective_id=collective_id, has_side_effects=True
-        ),
-    )(x)
 
 
 def factors(n):
@@ -109,7 +65,7 @@
     return 2 * (major - 1) + (2 * major - 1) * 2 * (minor // 2)
 
 
-def start_gather(n, w_ref, out_ref, send, recv, between):
+def start_gather(n, w_ref, out_ref, send, recv, between, done):
     major, minor = factors(n)
     me = lax.axis_index("table")
     row, place = me // minor, snake(me % minor)
@@ -177,76 +133,190 @@
     flight = line_go(1)
     rings = [ring_go(row, True, None, 1)]
     between(0)
+
+    def forward(i, step):
+        block, own, present = blocks[i]
+        for copy in rings[i]:
+            when(present)(copy.wait_recv)
+        if step < minor // 2:
+            rings[i] = ring_go(block, own, present, step + 1)
+        else:
+            when(present)(functools.partial(done, block))
+
+    ready = 0
     for step in range(1, major):
         for present, copy in flight:
             pl.when(present)(copy.wait_recv)
         if step + 1 < major:
             flight = line_go(step + 1)
+        known = len(blocks)
         for way in (1, -1):
             block = lax.rem(row - way * step + major, major)
             blocks.append((block, False, has(-way * step)))
             rings.append(ring_go(*blocks[-1], 1))
         between(step)
+        if minor // 2 > 1:
+            for i in range(ready, known):
+                forward(i, 1)
+            ready = known
     for step in range(1, minor // 2 + 1):
-        for i, (block, own, present) in enumerate(blocks):
-            for copy in rings[i]:
-                when(present)(copy.wait_recv)
-            if step < minor // 2:
-                rings[i] = ring_go(block, own, present, step + 1)
+        for i in range(len(blocks)):
+            if step > 1 or minor // 2 == 1 or i >= ready:
+                forward(i, step)
     return [(when(present), copy) for present, copy in sends]
 
 
-def gather_kernel(n, w_ref, x_ref, w_out, y_ref, hold_w, hold_x, ws, wr, xs, xr, local):
+def rows_of(ref, d, capacity):
+    return ref.at[:, pl.ds(pl.multiple_of(d * capacity, capacity), capacity)]
+
+
+def gather_kernel(
+    n, w_ref, asks_ref, table_ref, cot_ref,
+    w_out, asked_out, y_ref, grad_ref,
+    w_all, asked, table, looked, ws, wr, qs, qr, xs, xr, ts, local,
+):
     greet_table(n)
+    major, minor = factors(n)
     me = lax.axis_index("table")
     depth = w_ref.shape[0]
-    load = pltpu.make_async_copy(w_ref, hold_w, local.at[2])
-    load.start()
-    copies = exchange_copies(n, x_ref, y_ref, xs, xr, second_window)
-    share = -(-(n - 1) // factors(n)[0])
+    ngram, rows, width = table_ref.shape
+    capacity = looked.shape[1] // n
+    own_rows = pl.ds(pl.multiple_of(me * depth, depth), depth)
+    loads = [
+        pltpu.make_async_copy(table_ref.at[k], table.at[k], ts.at[k]) for k in range(ngram)
+    ]
+    keep = pltpu.make_async_copy(w_ref, w_all.at[own_rows], local.at[0])
+    questions = exchange_copies(n, asks_ref, asked, qs, qr, first_window)
+    for copy in questions:
+        copy.start()
+    for load in loads:
+        load.start()
+    keep.start()
+    asked[me] = asks_ref[me]
+
+    near, far = [], []
+    for along in range(major):
+        for across in range(minor):
+            if along == 0 and across == 0:
+                continue
+            to = lax.rem(me // minor + along, major) * minor + lax.rem(me + across, minor)
+            spot = along * minor + across
+            (far if along else near).append(
+                pltpu.make_async_remote_copy(
+                    src_ref=rows_of(looked, to, capacity),
+                    dst_ref=rows_of(y_ref, me, capacity),
+                    send_sem=xs.at[spot],
+                    recv_sem=xr.at[spot],
+                    device_id={"table": to},
+                    device_id_type=MESH,
+                )
+            )
+    mine = pltpu.make_async_copy(
+        rows_of(looked, me, capacity), rows_of(y_ref, me, capacity), local.at[1]
+    )
+    group = 128 // capacity
+    tile = width // 4
+
+    def look_up():
+        for copy in questions:
+            copy.wait_recv()
+        for load in loads:
+            load.wait()
+        for q in range(n // group):
+            for k in range(ngram):
+                wanted = asked[q * group, k : k + 1, :]
+                for i in range(1, group):
+                    wanted = wanted + asked[q * group + i, k : k + 1, :]
+                place = lax.broadcasted_iota(jnp.int32, (rows, 128), 0) + 1
+                hit = (place == wanted).astype(jnp.float32).astype(jnp.bfloat16)
+
+                @pl.loop(0, 4)
+                def _(c):
+                    columns = pl.ds(pl.multiple_of(c * tile, tile), tile)
+                    found = lax.dot_general(
+                        hit,
+                        table[k, :, columns],
+                        (((0,), (0,)), ((), ())),
+                        preferred_element_type=jnp.float32,
+                    )
+                    looked[k, q * 128 : (q + 1) * 128, columns] = found.astype(looked.dtype)
 
     def between(i):
-        for copy in copies[i * share : (i + 1) * share]:
-            copy.start()
-
-    started = start_gather(n, w_ref, w_out, ws, wr, between)
-    load.wait()
-    put = pltpu.make_async_copy(
-        hold_w, w_out.at[pl.ds(pl.multiple_of(me * depth, depth), depth)], local.at[3]
-    )
-    put.start()
-    store = own_block(x_ref, y_ref, hold_x, local, second_window)
-    store.wait()
-    put.wait()
-    for copy in copies:
+        if i == 0:
+            look_up()
+            mine.start()
+            for copy in near:
+                copy.start()
+        if i == major - 2:
+            for copy in far:
+                copy.start()
+
+    span = minor * depth
+    chunk = min(512, span)
+    puts = []
+
+    def done(block):
+        at = pl.ds(pl.multiple_of(block * span, span), span)
+        put = pltpu.make_async_copy(w_all.at[at], w_out.at[at], local.at[2 + block])
+        put.start()
+
+        @pl.loop(0, span // chunk)
+        def _(c):
+            some = pl.ds(pl.multiple_of(block * span + c * chunk, chunk), chunk)
+            grad_ref[:, some] = lax.dot_general(
+                cot_ref[...],
+                w_all[some, :],
+                (((1,), (1,)), ((), ())),
+                preferred_element_type=jnp.float32,
+            )
+
+    keep.wait()
+    started = start_gather(n, w_ref, w_all, ws, wr, between, done)
+    for copy in questions:
+        copy.wait_send()
+    asked_out[...] = asked[...]
+    mine.wait()
+    for copy in near + far:
         copy.wait()
     for when, copy in started:
         when(copy.wait_send)
-
-
-def gather_and_exchange(w, x, n, collective_id):
+    for block in range(major):
+        at = pl.ds(block * span, span)
+        pltpu.make_async_copy(w_all.at[at], w_out.at[at], local.at[2 + block]).wait()
+
+
+def gather_and_exchange(w, asks, table, cot, capacity, n, collective_id):
     steps = gather_steps(n)
+    ngram, _, width = table.shape
+    whole = pl.BlockSpec(memory_space=pltpu.VMEM)
     return pl.pallas_call(
         functools.partial(gather_kernel, n),
         out_shape=(
             jax.ShapeDtypeStruct((n * w.shape[0], w.shape[1]), w.dtype),
-            jax.ShapeDtypeStruct(x.shape, x.dtype),
-        ),
-        in_specs=[ANY, ANY],
-        out_specs=(ANY, ANY),
+            jax.ShapeDtypeStruct(asks.shape, asks.dtype),
+            jax.ShapeDtypeStruct((ngram, n * capacity, width), table.dtype),
+            jax.ShapeDtypeStruct((cot.shape[0], n * w.shape[0]), jnp.float32),
+        ),
+        in_specs=[ANY, whole, ANY, whole],
+        out_specs=(ANY, whole, ANY, whole),
         scratch_shapes=[
-            pltpu.VMEM(w.shape, w.dtype),
-            pltpu.VMEM(x.shape[:1] + x.shape[2:], x.dtype),
+            pltpu.VMEM((n * w.shape[0], w.shape[1]), w.dtype),
+            pltpu.VMEM(asks.shape, asks.dtype),
+            pltpu.VMEM(table.shape, table.dtype),
+            pltpu.VMEM((ngram, n * capacity, width), table.dtype),
             pltpu.SemaphoreType.DMA((steps,)),
             pltpu.SemaphoreType.DMA((steps,)),
             pltpu.SemaphoreType.DMA((n,)),
             pltpu.SemaphoreType.DMA((n,)),
-            pltpu.SemaphoreType.DMA((4,)),
+            pltpu.SemaphoreType.DMA((n,)),
+            pltpu.SemaphoreType.DMA((n,)),
+            pltpu.SemaphoreType.DMA((ngram,)),
+            pltpu.SemaphoreType.DMA((2 + factors(n)[0],)),
         ],
         compiler_params=pltpu.CompilerParams(
             collective_id=collective_id, has_side_effects=True
         ),
-    )(w, x)
+    )(w, asks, table, cot)
 
 
 def greet_pair():
@@ -346,22 +416,21 @@
         slot = owner * capacity + slot_rank(owner, groups)
         mark = slot[:, None] == places[None, :]
         marks.append(mark)
-        wanted = jnp.sum(jnp.where(mark, hash_offset[k][:, None] + 1, 0), axis=0) - 1
+        wanted = jnp.sum(jnp.where(mark, hash_offset[k][:, None] + 1, 0), axis=0)
         requests.append(wanted.reshape(groups, capacity))
-    stacked = jnp.stack(requests, axis=1)
-    lanes = -(-capacity // 128) * 128
+    shared = 128 // capacity
+    lane = jnp.arange(128, dtype=jnp.int32)
+    stacked = jnp.tile(jnp.stack(requests, axis=1), (1, 1, shared))
+    stacked = jnp.where(lane // capacity == lax.axis_index("table") % shared, stacked, 0)
     levels = -(-ngram // 8) * 8
-    stacked = jnp.pad(stacked, ((0, 0), (0, levels - ngram), (0, lanes - capacity)))
-    asked = exchange(stacked, groups, first_window, 0)[:, :ngram, :capacity]
+    stacked = jnp.pad(stacked, ((0, 0), (0, levels - ngram), (0, 0)))
+    weight, asked, fetched, partial_grad = gather_and_exchange(
+        proj_weight, stacked, hash_tables, cotangent, capacity, groups, 1
+    )
+    asked = jnp.sum(asked.reshape(groups // shared, shared, levels, 128)[:, :, :ngram], axis=1) - 1
     asked = jnp.transpose(asked, (1, 0, 2)).reshape(ngram, span)
     rows = jnp.arange(rows_dev, dtype=jnp.int32)
     hits = (asked[:, :, None] == rows[None, None, :]).astype(jnp.bfloat16)
-    looked = lax.dot_general(
-        hits, hash_tables, (((2,), (1,)), ((0,), (0,))), preferred_element_type=jnp.float32
-    ).astype(jnp.bfloat16)
-    weight, fetched = gather_and_exchange(
-        proj_weight, looked.reshape(ngram, groups, capacity, width), groups, 1
-    )
 
     mark = jnp.concatenate(marks, axis=1).astype(jnp.bfloat16)
     codes = jnp.arange(byte_table.shape[0], dtype=jnp.int32)
@@ -376,9 +445,6 @@
     total = jnp.sum(full * full, axis=1)
     scale = lax.rsqrt(total / full_width + eps)[:, None]
     normed = (full * scale * gain[None, :]).astype(jnp.bfloat16)
-    partial_grad = lax.dot_general(
-        cotangent, weight, (((1,), (1,)), ((), ())), preferred_element_type=jnp.float32
-    )
     inner_part = jnp.sum(full * (partial_grad * gain[None, :]), axis=1, keepdims=True)
     other_grad, other_inner = swap_halves(
         partial_grad, jnp.broadcast_to(inner_part, (tokens, 128)), 3

time: 419 us -> 338 us (0.81)
  starting transfers between devices: 61.1 us -> 6.77 us
  matrix products: 53.3 us -> 24.8 us
  other arithmetic: 3.82 us -> 8.51 us
    all_to_all x1, starting transfers between devices: 61.1 us -> 6.77 us  [on_device(): lax.all_to_all(outgoing.reshape(ngram, groups, capacity, width), 'table',...]
    dot_general x2 -> x0, matrix products: 28.4 us -> none  [the longest x1 18.9 us: on_device(): lax.dot_general(cotangent, weight, (((1,), (1,)), ((), ())), preferred_el...]
    pallas_call x1 -> x0, Pallas kernels: 8.21 us -> none  [exchange(): pl.pallas_call(functools.partial(exchange_kernel, n, window), out_shape=j...]
    pallas_call x1, Pallas kernels: 187 us -> 195 us  [gather_and_exchange(): pl.pallas_call(functools.partial(gather_kernel, n), out_shape=(jax.ShapeD...]
    reduce_sum x2 -> x4, other arithmetic: 0.3 us -> 4.97 us  [the longest x1 3.82 us: on_device(): jnp.sum(full * (partial_grad * gain[None, :]), axis=1, keepdims=True)]
  transfers between devices with their start and end apart: 1 -> 1, of which waited for: 1 -> 1; matrix products, arithmetic and copies ran while one was open for 2% -> 3% of each run, Pallas kernels for 0% -> 0%
where the time goes in v3:
time: 338 us
  Pallas kernels  203 us (60%)
  waiting for transfers between devices  85.8 us (25%)
  matrix products  24.8 us (7%)
  other arithmetic  8.51 us (3%)
  local copies, waits for them, and re-layouts  7.77 us (2%)
  starting transfers between devices  6.77 us (2%)
    pallas_call x1, Pallas kernels, gather_and_exchange(): pl.pallas_call(functools.partial(gather_kernel, n), out_shape=(jax.ShapeD...  195 us
    all_to_all x1, waiting for transfers between devices, on_device(): lax.all_to_all(outgoing.reshape(ngram, groups, capacity, width), 'table',...  85.8 us
    dot_general x1, matrix products, on_device(): jnp.dot(normed, weight, preferred_element_type=jnp.float32)  9.29 us
    all_to_all x1, starting transfers between devices, on_device(): lax.all_to_all(outgoing.reshape(ngram, groups, capacity, width), 'table',...  6.77 us
  transfers between devices with their start and end apart: 1, of which 1 were waited for; matrix products, arithmetic and copies ran while one was open for 3% of the time, Pallas kernels for 0%

profile of v3, /device:TPU:14, one launch (start us, length us, event | category | flops | bytes accessed | tf_op | source)
XLA Modules:
  0.0 338.0 jit_solution(2752345481423717590)
XLA Ops:
  0.7 0.8 slice_add_fusion.1
  1.4 0.7 fusion.26
  2.2 0.6 reduce-window.16
  2.7 0.2 slice_reduce_fusion.1
  3.3 0.6 reduce-window.14
  3.9 0.2 slice_reduce_fusion.2
  4.2 0.2 iota_compare_fusion.2
  4.9 0.6 pad.4.asks_ref
  5.5 194.7 %shard_map.95 = (bf16[4096,2048]{1,0:T(8,128)(2,1)}, s32[16,8,128]{2,1,0:T(8,128)}, bf16[2,512,2048]{2,1,0:T(8,128)(2,1)}, f32[256,4096]{1,0:T(8,128)}) custom-call(bf16[256,2048]{1,0:T(8,128)(2,1)} %w_ref.1, s32[16,8,128]{2,1,0:T(8,128)} %pad.4.asks_ref, bf16[2,1024,2048]{2,1,0:T(8,128)(2,1)} %table_ref.1, bf16[256,2048]{1,0:T(8,128)(2,1)} %cot_ref.1), custom_call_target="tpu_custom_call" | custom-call | tf_op jit(solution)/shard_map/pallas_call | solution.py:292
  200.2 3.4 %fusion.12 = f32[256,2048]{1,0:T(8,128)S(1)} fusion(bf16[1024,2048]{1,0:T(8,128)(2,1)} %bitcast.69, pred[256,512]{1,0:T(32,128)(4,1)S(1)} %get-tuple-element.20, pred[256,512]{1,0:T(32,128)(4,1)S(1)} %get-tuple-element.21), kind=kOutput, calls=%fused_computation.25 | convolution fusion | flops 1074003968 | bytes 6553600 | tf_op jit(solution)/shard_map/dot_general | solution.py:439
  203.7 1.5 fusion.4.x_ref
  205.2 4.0 %shard_map.96 = bf16[256,4096]{1,0:T(8,128)(2,1)} custom-call(bf16[256,2048]{1,0:T(8,128)(2,1)} %fusion.4.x_ref), custom_call_target="tpu_custom_call" | custom-call | tf_op jit(solution)/shard_map/pallas_call | solution.py:350
  209.3 3.8 %fusion.3 = (f32[256]{0:T(256)S(1)}, f32[256]{0:T(256)S(1)}) fusion(bf16[256,4096]{1,0:T(8,128)(2,1)} %shard_map.96, f32[256,4096]{1,0:T(8,128)} %get-tuple-element.11.part_ref, f32[4096]{0:T(1024)S(1)} %copy-done.4), kind=kLoop, calls=%fused_computation.7 | loop fusion | flops 6290944 | bytes 6309888 | tf_op jit(solution)/shard_map/reduce_sum | solution.py:448
  213.1 0.8 broadcast_in_dim.52.side_ref
  213.8 4.7 %shard_map.97 = (f32[256,2048]{1,0:T(8,128)}, f32[256,128]{1,0:T(8,128)}) custom-call(f32[256,4096]{1,0:T(8,128)} %get-tuple-element.11.part_ref, f32[256,128]{1,0:T(8,128)} %broadcast_in_dim.52.side_ref), custom_call_target="tpu_custom_call" | custom-call | tf_op jit(solution)/shard_map/pallas_call | solution.py:386
  218.7 1.0 multiply_reduce_fusion
  219.8 3.8 %convolution_convert_fusion.1 = bf16[1024,2048]{1,0:T(8,128)(2,1)S(1)} fusion(bf16[256,2048]{1,0:T(8,128)(2,1)S(1)} %copy-done.2, f32[256,2048]{1,0:T(8,128)} %get-tuple-element.12, f32[256,4096]{1,0:T(8,128)} %get-tuple-element.11.part_ref, s32[]{:T(128)S(6)} %select_n.32, f32[256]{0:T(256)S(1)} %multiply_reduce_fusion, f32[2048]{0:T(1024)S(1)} %dynamic_slice.7, ...), kind=kOutput, calls=%fused_computation.9 | convolution fusion | flops 1081344000 | bytes 9709572 | tf_op jit(solution)/shard_map/dot_general | solution.py:458
  223.6 2.3 copy.21
  225.9 6.8 %all-to-all-start = ((bf16[2,16,32,2048]{3,2,0,1:T(8,128)(2,1)}), bf16[2,16,32,2048]{3,2,0,1:T(8,128)(2,1)}, u32[]{:S(2)}, u32[]{:S(2)}) async-start(bf16[2,16,32,2048]{3,2,0,1:T(8,128)(2,1)} %copy.21), calls=%async_computation | async-start | bytes 8388608 | tf_op jit(solution)/shard_map/all_to_all | solution.py:461
  232.7 0.9 slice_reduce_fusion
  233.6 9.3 %convolution_convert_fusion.2 = bf16[256,2048]{1,0:T(8,128)(2,1)} fusion(bf16[4096,2048]{1,0:T(8,128)(2,1)} %get-tuple-element.9, bf16[256,4096]{1,0:T(8,128)(2,1)S(1)} %copy-done.3, f32[4096]{0:T(1024)S(1)} %copy-done.4, f32[256]{0:T(256)S(1)} %add_rsqrt_fusion), kind=kOutput, calls=%fused_computation.11 | convolution fusion | flops 4299685888 | bytes 19940352 | tf_op jit(solution)/shard_map/dot_general | solution.py:474
  242.9 85.8 %all-to-all-done = bf16[2,16,32,2048]{3,2,0,1:T(8,128)(2,1)} async-done(((bf16[2,16,32,2048]{3,2,0,1:T(8,128)(2,1)}), bf16[2,16,32,2048]{3,2,0,1:T(8,128)(2,1)}, u32[]{:S(2)}, u32[]{:S(2)}) %all-to-all-start) | async-done | bytes 4194336 | tf_op jit(solution)/shard_map/all_to_all | solution.py:461
  328.7 2.5 copy.22
  331.2 6.8 %convolution_convert_fusion = bf16[2,1024,2048]{2,1,0:T(8,128)(2,1)} fusion(bf16[2,512,2048]{2,1,0:T(8,128)(2,1)S(1)} %bitcast.58, s32[2,512]{1,0:T(2,128)S(1)} %add_bitcast_fusion.2), kind=kOutput, calls=%fused_computation.3 | convolution fusion | flops 4300210176 | bytes 12587008 | tf_op jit(solution)/shard_map/dot_general | solution.py:468
  (35 shorter events, 1.1 us)
Async XLA Ops:
  0.6 203.1 %copy-start = (bf16[256,2048]{1,0:T(8,128)(2,1)S(1)}, bf16[256,2048]{1,0:T(8,128)(2,1)}, u32[]{:S(2)}) copy-start(bf16[256,2048]{1,0:T(8,128)(2,1)} %param.9) | copy-start | bytes 3145732
  200.2 3.5 %copy-start.5 = (s32[256]{0:T(256)S(1)}, s32[256]{0:T(256)}, u32[]{:S(2)}) copy-start(s32[256]{0:T(256)} %param.10) | copy-start | bytes 3076
  203.7 5.5 %copy-start.4 = (f32[4096]{0:T(1024)S(1)}, f32[4096]{0:T(1024)}, u32[]{:S(2)}) copy-start(f32[4096]{0:T(1024)} %param.13) | copy-start | bytes 49156
  209.2 10.5 %copy-start.2 = (bf16[256,2048]{1,0:T(8,128)(2,1)S(1)}, bf16[256,2048]{1,0:T(8,128)(2,1)}, u32[]{:S(2)}) copy-start(bf16[256,2048]{1,0:T(8,128)(2,1)} %fusion.4.x_ref) | copy-start | bytes 3145732
  225.9 7.6 %copy-start.3 = (bf16[256,4096]{1,0:T(8,128)(2,1)S(1)}, bf16[256,4096]{1,0:T(8,128)(2,1)}, u32[]{:S(2)}) copy-start(bf16[256,4096]{1,0:T(8,128)(2,1)} %shard_map.96) | copy-start | bytes 6291460
  225.9 102.8 %all-to-all-start = ((bf16[2,16,32,2048]{3,2,0,1:T(8,128)(2,1)}), bf16[2,16,32,2048]{3,2,0,1:T(8,128)(2,1)}, u32[]{:S(2)}, u32[]{:S(2)}) async-start(bf16[2,16,32,2048]{3,2,0,1:T(8,128)(2,1)} %copy.21), calls=%async_computation | async-start | bytes 8388608 | tf_op jit(solution)/shard_map/all_to_all | solution.py:461
  331.2 6.8 %copy-start.1 = (bf16[256,2048]{1,0:T(8,128)(2,1)S(1)}, bf16[256,2048]{1,0:T(8,128)(2,1)}, u32[]{:S(2)}) copy-start(bf16[256,2048]{1,0:T(8,128)(2,1)} %param.9) | copy-start | bytes 3145732
